TPU v7x, 256 devices: a whole 4x4x8 slice. The times are simulated.
256 devices in a mesh: tm: 16 (over z, core), pts: 16 (over x, y).
Axes of the slice: x: 4, y: 4, z: 8, core: 2. Of those that a mesh axis runs over, the one named last changes fastest.
Arguments:
- snapshots: float32 [1024, 131072], P('tm', 'pts'), may hold values from -110 to 110
- weights: float32 [131072], P(('pts', 'tm')), may hold values from 0.25 to 12, as said below
Outputs:
- modes: float32 [2, 33, 31, 131072], P(None, None, None, ('pts', 'tm'))
- triangle: float32 [2, 33, 31, 31], replicated
Inputs may be any that keep to these rules, and one draw needn't show every extreme that they name: Positive weights.
All inputs are finite; a program needn't handle non-finite values.
Results may differ from a plain program's by a relative error of at most 0.00065.
Values sent between devices are 32-bit elements; how exact they have to be, the bound alone decides.
A program may use at most 128 MiB of HBM per device.

v0:
```python
import jax
import jax.numpy as jnp
import ml_dtypes
import numpy as np
from jax import lax
from jax.experimental import pallas as pl
from jax.experimental.pallas import tpu as pltpu
from jax.sharding import PartitionSpec as P

SEG = 64
HOP = 32
NF = 33
NT = 1024
NB = 31
MESH = pl.DeviceIdType.MESH

VMEM = pl.BlockSpec(memory_space=pltpu.VMEM)
TILE = 32
SLOTS = 32


def fourier_table():
    sample = np.arange(SEG)[:, None]
    column = np.arange(SEG)[None, :]
    frequency = np.where(column < NF, column, column - HOP)
    window = 0.5 - 0.5 * np.cos(2.0 * np.pi * sample / SEG)
    phase_angle = 2.0 * np.pi * ((frequency * sample) % SEG) / SEG
    waveform = np.where(column < NF, np.cos(phase_angle), -np.sin(phase_angle))
    return (waveform * window / np.sqrt(3 * SEG / 8)).astype(np.float32)


def table_parts():
    table = fourier_table().T
    high = table.astype(ml_dtypes.bfloat16)
    rest = table - high.astype(np.float32)
    middle = rest.astype(ml_dtypes.bfloat16)
    low = (rest - middle.astype(np.float32)).astype(ml_dtypes.bfloat16)
    return np.concatenate([high, high, middle, high, middle, low], axis=1)


def parts_of(value, count):
    parts = []
    for _ in range(count):
        part = value.astype(jnp.bfloat16)
        parts.append(part)
        value = value - part.astype(jnp.float32)
    return parts


def left6(value):
    high, middle, low = parts_of(value, 3)
    return jnp.concatenate([high, high, middle, high, middle, low], axis=1)


def right6(value):
    high, middle, low = parts_of(value, 3)
    return jnp.concatenate([high, middle, high, low, middle, high], axis=0)


def left3(value):
    high, low = parts_of(value, 2)
    return jnp.concatenate([high, high, low], axis=1)


def right3(value):
    high, low = parts_of(value, 2)
    return jnp.concatenate([high, low, high], axis=0)


def multiply(left, right):
    return jnp.dot(left, right, preferred_element_type=jnp.float32)


def self_product(value, count):
    stacked = jnp.concatenate(parts_of(value, count), axis=0)
    whole = lax.dot_general(
        stacked, stacked, (((1,), (1,)), ((), ())), preferred_element_type=jnp.float32
    )
    size = value.shape[0]
    rows = sum(whole[i * size : (i + 1) * size] for i in reversed(range(count)))
    return sum(rows[:, i * size : (i + 1) * size] for i in reversed(range(count)))


def gram_tile(product, slot):
    top_left = product[:TILE, :TILE]
    bottom_right = product[TILE:, TILE:]
    row = lax.broadcasted_iota(jnp.int32, (TILE, TILE), 0)
    column = lax.broadcasted_iota(jnp.int32, (TILE, TILE), 1)
    if slot == 0:
        return jnp.where(column >= row, top_left, pltpu.roll(bottom_right, 1, 0))
    imaginary = product[:TILE, TILE:] - product[TILE:, :TILE]
    return jnp.where(column >= row, top_left + bottom_right, imaginary)


def put_tiles(out, group, tiles):
    joined = jnp.concatenate(tiles, axis=1)
    out[2 * group] = joined[:16]
    out[2 * group + 1] = joined[16:]


def slot_rows(spectrum, slot):
    halves = [
        [
            spectrum[panel, pl.ds(slot + half, TILE, stride=SEG), :]
            for panel in range(spectrum.shape[0])
        ]
        for half in (0, 32)
    ]
    return jnp.concatenate([jnp.concatenate(row, axis=1) for row in halves], axis=0)


def spectrum_kernel(records, weights, table, spectrum, packed):
    root = jnp.sqrt(weights[...])

    def block(b, carry):
        rows = records[pl.ds(pl.multiple_of(HOP * b, HOP), SEG), :]
        lines = pl.ds(pl.multiple_of(SEG * b, SEG), SEG)
        value = multiply(table[...], right6(rows)) * root
        for panel in range(spectrum.shape[0]):
            spectrum[panel, lines, :] = value[:, 128 * panel : 128 * (panel + 1)]
        return carry

    lax.fori_loop(0, NB, block, 0, unroll=True)
    for panel in range(spectrum.shape[0]):
        spectrum[panel, NB * SEG :, :] = jnp.zeros((SEG, 128), jnp.float32)
    for group in range(8):
        tiles = []
        for slot in range(group, SLOTS, 8):
            value = slot_rows(spectrum, slot)
            tiles.append(gram_tile(self_product(value, 3), slot))
        put_tiles(packed, group, tiles)


def spectra(records, weights):
    points = records.shape[1]
    return pl.pallas_call(
        spectrum_kernel,
        out_shape=(
            jax.ShapeDtypeStruct((points // 128, TILE * SEG, 128), jnp.float32),
            jax.ShapeDtypeStruct((16, 16, 128), jnp.float32),
        ),
        in_specs=[VMEM] * 3,
        out_specs=(VMEM, VMEM),
        compiler_params=pltpu.CompilerParams(vmem_limit_bytes=48 << 20),
        name="spectra",
    )(records, weights.reshape(1, points), jnp.asarray(table_parts()))


def sum_kernel(x_ref, o_ref, half, part, total, share, full, *sems):
    send0, recv0, send1, recv1, send2, recv2, send3, recv3, send4, recv4 = sems
    me_p = lax.axis_index("pts")
    me_t = lax.axis_index("tm")
    core = lax.rem(me_t, 2)
    chip = me_t // 2
    n = part.shape[0]
    chips = share.shape[0]
    other = {"tm": me_t + 1 - 2 * core}
    own_lines = pl.ds(pl.multiple_of(8 * core, 8), 8)
    other_lines = pl.ds(pl.multiple_of(8 - 8 * core, 8), 8)

    def ahead(d):
        return lax.rem(me_p + d, n)

    def remote(source, target, send, recv, device):
        return pltpu.make_async_remote_copy(
            src_ref=source, dst_ref=target, send_sem=send, recv_sem=recv,
            device_id=device, device_id_type=MESH,
        )

    def along(d):
        return {"tm": lax.rem(me_t + 2 * d, 2 * chips)}

    swap = remote(x_ref.at[:, other_lines, :], half, send0, recv0, other)

    def scatter(d):
        return remote(
            full.at[ahead(d)], part.at[d], send1.at[d], recv1.at[d], {"pts": ahead(d)}
        )

    def exchange(d):
        return remote(total, share.at[chip], send2.at[d], recv2.at[d], along(d))

    def gather(d):
        return remote(
            total, o_ref.at[me_p, own_lines, :], send3.at[d], recv3.at[d], {"pts": ahead(d)}
        )

    back = remote(
        o_ref.at[:, own_lines, :], o_ref.at[:, own_lines, :], send4, recv4, other
    )

    def each(count, action):
        def step(d, carry):
            action(d)
            return carry

        lax.fori_loop(1, count, step, 0)

    barrier = pltpu.get_barrier_semaphore()

    def greet(device):
        pl.semaphore_signal(barrier, inc=1, device_id=device, device_id_type=MESH)

    greet(other)
    each(n, lambda d: greet({"pts": ahead(d)}))
    each(chips, lambda d: greet(along(d)))
    pl.semaphore_wait(barrier, n + chips - 1)

    swap.start()
    swap.wait()
    full[...] = x_ref[:, own_lines, :] + half[...]
    each(n, lambda d: scatter(d).start())
    part[0] = full[me_p]
    each(n, lambda d: scatter(d).wait())
    total[...] = jnp.sum(part[...], axis=0)
    each(chips, lambda d: exchange(d).start())
    share[chip] = total[...]
    each(chips, lambda d: exchange(d).wait())
    total[...] = jnp.sum(share[...], axis=0)
    each(n, lambda d: gather(d).start())
    o_ref[me_p, own_lines, :] = total[...]
    each(n, lambda d: gather(d).wait())
    back.start()
    back.wait()


def global_sum(packed):
    n, lines, lanes = packed.shape
    chips = lax.axis_size("tm") // 2
    dma = pltpu.SemaphoreType.DMA
    buffer = pltpu.VMEM((n, lines // 2, lanes), jnp.float32)
    return pl.pallas_call(
        sum_kernel,
        out_shape=jax.ShapeDtypeStruct(packed.shape, packed.dtype),
        in_specs=[VMEM],
        out_specs=VMEM,
        scratch_shapes=[
            buffer,
            buffer,
            pltpu.VMEM((lines // 2, lanes), jnp.float32),
            pltpu.VMEM((chips, lines // 2, lanes), jnp.float32),
            buffer,
            dma, dma, dma((n,)), dma((n,)), dma((chips,)), dma((chips,)),
            dma((n,)), dma((n,)), dma, dma,
        ],
        compiler_params=pltpu.CompilerParams(collective_id=0, has_side_effects=True),
        name="global_sum",
    )(packed)


def factor_lanes(scale, packed, tiles, state_real, state_imag):
    column = lax.broadcasted_iota(jnp.int32, (TILE, 128), 0)
    lane = lax.broadcasted_iota(jnp.int32, (TILE, 128), 1)
    for b in range(TILE):
        lines = packed[pl.ds(b, 8, stride=TILE), :]
        spread = jnp.concatenate(
            [lines] + [pltpu.roll(lines, 128 - 32 * s, 1) for s in (1, 2, 3)]
            + [jnp.zeros((96, 128), jnp.float32)],
            axis=0,
        )
        tiles[b * TILE : (b + 1) * TILE, :] = jnp.transpose(spread)[:TILE] * scale
    tiles[TILE * TILE :, :] = jnp.zeros((TILE, 128), jnp.float32)
    for b in range(NB):
        straight = tiles[b * TILE : (b + 1) * TILE, :]
        turned = tiles[pl.ds(b, TILE, stride=TILE), :]
        below = tiles[(b + 1) * TILE : (b + 2) * TILE, :]
        below_turned = tiles[pl.ds(TILE + b, TILE, stride=TILE), :]
        last = pltpu.roll(jnp.where(column <= b, below, below_turned), 32, 1)
        real = jnp.where(column >= b, straight, turned)
        real = jnp.where(lane == 32, last, real)
        imag = jnp.where(column < b, straight, -turned)
        state_real[b] = jnp.where(lane > 32, jnp.where(column == b, 1.0, 0.0), real)
        state_imag[b] = jnp.where(
            (lane == 0) | (lane >= 32) | (column == b), 0.0, imag
        )
    for k in range(NB):
        here = column == k
        inverse = 1.0 / jnp.sqrt(state_real[k, k : k + 1, :])
        row_real = jnp.where(here, inverse, state_real[k] * inverse)
        row_imag = jnp.where(here, 0.0, state_imag[k] * inverse)
        state_real[k] = row_real
        state_imag[k] = row_imag

        def eliminate(i, carry):
            pick_real = state_real[k, pl.ds(i, 1), :]
            pick_imag = state_imag[k, pl.ds(i, 1), :]
            work_real = jnp.where(here, 0.0, state_real[i])
            work_imag = jnp.where(here, 0.0, state_imag[i])
            state_real[i] = work_real - (pick_real * row_real + pick_imag * row_imag)
            state_imag[i] = work_imag - (pick_real * row_imag - pick_imag * row_real)
            return carry

        lax.fori_loop(k + 1, NB, eliminate, 0, unroll=True)


def write_inverse(state_real, state_imag, inverse):
    column = lax.broadcasted_iota(jnp.int32, (TILE, 128), 0)
    lane = lax.broadcasted_iota(jnp.int32, (TILE, 128), 1)
    for k in range(NB):
        keep = column <= k
        real = jnp.where(keep, state_real[k], 0.0)
        imag = jnp.where(keep, state_imag[k], 0.0)
        lower = jnp.where(lane == 0, pltpu.roll(real, 96, 1), real)
        joined = jnp.concatenate([real, imag, -imag, lower], axis=0)
        inverse[40 * k : 40 * (k + 1), :] = jnp.transpose(joined)[:40]
    inverse[40 * NB :, :] = jnp.zeros((40, 128), jnp.float32)


def factor_kernel(scale, packed, inverse, state_real, state_imag, tiles):
    factor_lanes(scale, packed, tiles, state_real, state_imag)
    write_inverse(state_real, state_imag, inverse)


STATE = jax.ShapeDtypeStruct((NB, TILE, 128), jnp.float32)
INVERSE = jax.ShapeDtypeStruct((TILE * 40, 128), jnp.float32)


def factor(packed, points_total):
    return pl.pallas_call(
        lambda *refs: factor_kernel(1.0 / points_total, *refs),
        out_shape=(INVERSE, STATE, STATE),
        in_specs=[VMEM],
        out_specs=(VMEM,) * 3,
        scratch_shapes=[pltpu.VMEM(((TILE + 1) * TILE, 128), jnp.float32)],
        compiler_params=pltpu.CompilerParams(vmem_limit_bytes=48 << 20),
        name="factor",
    )(packed.reshape(256, 128))


def finish_kernel(
    scale, packed, first_real, first_imag, inverse, triangle_real, triangle_imag,
    tiles, state_real, state_imag, right_real, right_imag,
):
    factor_lanes(scale, packed, tiles, state_real, state_imag)
    write_inverse(state_real, state_imag, inverse)
    column = lax.broadcasted_iota(jnp.int32, (TILE, 128), 0)
    for k in range(NB):
        real = first_real[k]
        diagonal = jnp.where(column == k, 1.0 / real, 0.0)
        right_real[k] = jnp.where(column > k, real, diagonal)
        right_imag[k] = jnp.where(column > k, first_imag[k], 0.0)
    for i in range(NB):
        own = 1.0 / state_real[i, i : i + 1, :]
        start = (own * right_real[i], own * right_imag[i])

        def gather(k, total):
            total_real, total_imag = total
            pick_real = state_real[i, pl.ds(k, 1), :]
            pick_imag = state_imag[i, pl.ds(k, 1), :]
            row_real = right_real[k]
            row_imag = right_imag[k]
            return (
                total_real + (pick_real * row_real - pick_imag * row_imag),
                total_imag + (pick_real * row_imag + pick_imag * row_real),
            )

        total_real, total_imag = lax.fori_loop(i + 1, NB, gather, start, unroll=True)
        triangle_real[i] = total_real
        triangle_imag[i] = total_imag


def finish(packed, first_real, first_imag, points_total):
    scratch = pltpu.VMEM(STATE.shape, jnp.float32)
    return pl.pallas_call(
        lambda *refs: finish_kernel(1.0 / points_total, *refs),
        out_shape=(INVERSE, STATE, STATE),
        in_specs=[VMEM] * 3,
        out_specs=(VMEM,) * 3,
        scratch_shapes=[pltpu.VMEM(((TILE + 1) * TILE, 128), jnp.float32)] + [scratch] * 4,
        compiler_params=pltpu.CompilerParams(vmem_limit_bytes=48 << 20),
        name="finish",
    )(packed.reshape(256, 128), first_real, first_imag)


def slot_matrix(inverse, slot):
    lines = inverse[pl.ds(slot, TILE, stride=40), :]
    return jnp.concatenate([lines[:, :64], lines[:, 64:]], axis=0)


def first_kernel(spectrum, inverse, ortho, packed):
    for group in range(8):
        tiles = []
        for slot in range(group, SLOTS, 8):
            value = slot_rows(spectrum, slot)
            value = multiply(left6(slot_matrix(inverse, slot)), right6(value))
            ortho[slot] = value
            tiles.append(gram_tile(self_product(value, 2), slot))
        put_tiles(packed, group, tiles)


def first_ortho(spectrum, inverse):
    points = spectrum.shape[0] * 128
    return pl.pallas_call(
        first_kernel,
        out_shape=(
            jax.ShapeDtypeStruct((SLOTS, SEG, points), jnp.float32),
            jax.ShapeDtypeStruct((16, 16, 128), jnp.float32),
        ),
        in_specs=[VMEM] * 2,
        out_specs=(VMEM, VMEM),
        compiler_params=pltpu.CompilerParams(vmem_limit_bytes=48 << 20),
        name="first_ortho",
    )(spectrum, inverse)


def modes_kernel(ortho, inverse, modes, held, sems):
    copies = []
    panels = ortho.shape[2] // 128
    step = 2 * panels

    def put(frequency, part, value):
        for panel in range(panels):
            held[frequency, pl.ds(2 * panel + part, NB, stride=step), :] = value[
                :NB, 128 * panel : 128 * (panel + 1)
            ]

    def send(frequency):
        copy = pltpu.make_async_copy(
            held.at[frequency], modes.at[frequency], sems.at[frequency]
        )
        copy.start()
        copies.append(copy)

    for slot in range(SLOTS):
        value = multiply(left3(slot_matrix(inverse, slot)), right3(ortho[slot]))
        put(slot, 0, value[:TILE])
        if slot:
            put(slot, 1, value[TILE:])
        else:
            nothing = jnp.zeros((TILE, value.shape[1]), jnp.float32)
            put(0, 1, nothing)
            put(NF - 1, 0, value[TILE:])
            put(NF - 1, 1, nothing)
            send(NF - 1)
        send(slot)
    for copy in copies:
        copy.wait()


def final_modes(ortho, inverse):
    points = ortho.shape[2]
    shape = (NF, NB * points // 64, 128)
    modes = pl.pallas_call(
        modes_kernel,
        out_shape=jax.ShapeDtypeStruct(shape, jnp.float32),
        in_specs=[VMEM] * 2,
        out_specs=pl.BlockSpec(memory_space=pl.ANY),
        scratch_shapes=[pltpu.VMEM(shape, jnp.float32), pltpu.SemaphoreType.DMA((NF,))],
        compiler_params=pltpu.CompilerParams(vmem_limit_bytes=48 << 20),
        name="modes",
    )(ortho, inverse)
    modes = modes.reshape(NF, NB, points // 128, 2, 128)
    return jnp.transpose(modes, (3, 0, 1, 2, 4)).reshape(2, NF, NB, points)


def shards(snapshots, weights):
    records = lax.all_to_all(snapshots, "tm", split_axis=1, concat_axis=0, tiled=True)
    points_total = weights.shape[0] * lax.axis_size("tm") * lax.axis_size("pts")
    spectrum, packed = spectra(records, weights)
    inverse, first_real, first_imag = factor(global_sum(packed), points_total)
    ortho, packed = first_ortho(spectrum, inverse)
    inverse, *triangle = finish(global_sum(packed), first_real, first_imag, points_total)
    triangle = jnp.stack([part[:, :NB, :NF] for part in triangle])
    return final_modes(ortho, inverse), jnp.transpose(triangle, (0, 3, 1, 2))


def solution(mesh):
    placed = (P("tm", "pts"), P(("pts", "tm")))
    return jax.shard_map(
        shards,
        mesh=mesh,
        in_specs=placed,
        out_specs=(P(None, None, None, ("pts", "tm")), P()),
        check_vma=False,
    )
```

profile of v0, /device:TPU:1, one launch (start us, length us, event | category | flops | bytes accessed | tf_op | source)
XLA Modules:
  0.0 147.6 jit_solution(1014969362718683807)
XLA Ops:
  0.6 0.0 copy-start.6
  0.6 0.0 copy-start.7
  0.7 1.8 %copy.10 = f32[8,16,8,512]{3,2,0,1:T(8,128)S(1)} copy(f32[8,16,8,512]{3,2,1,0:T(8,128)} %bitcast.27) | data formatting | bytes 4194304 | tf_op jit(solution)/shard_map/all_to_all | solution.py:457
  2.5 60.8 %all_to_all.19 = f32[64,16,512]{2,0,1:T(8,128)S(1)} all-to-all(f32[64,16,512]{2,0,1:T(8,128)S(1)} %bitcast.25), channel_id=1, replica_groups=mesh['tm'=16,'pts'=16] {'tm'}, dimensions={1} | all-to-all | bytes 4194304 | tf_op jit(solution)/shard_map/all_to_all | solution.py:457
  63.3 0.0 copy-done.6
  63.3 0.0 copy-done.7
  63.3 8.1 %spectra.1 = (f32[4,2048,128]{2,1,0:T(8,128)}, f32[16,16,128]{2,1,0:T(8,128)S(1)}) custom-call(f32[1024,512]{1,0:T(8,128)S(1)} %bitcast.21, f32[1,512]{1,0:T(1,128)S(1)} %bitcast.24, bf16[64,384]{1,0:T(8,128)(2,1)S(1)} %copy-done.6), custom_call_target="tpu_custom_call" | custom-call | tf_op jit(solution)/shard_map/spectra/pallas_call | solution.py:136
  71.4 0.0 copy-start.4
  71.4 0.7 copy-done.4
  72.0 23.2 %global_sum.2 = f32[16,16,128]{2,1,0:T(8,128)} custom-call(f32[16,16,128]{2,1,0:T(8,128)} %copy-done.4), custom_call_target="tpu_custom_call" | custom-call | tf_op jit(solution)/shard_map/global_sum/pallas_call | solution.py:232
  95.2 0.0 copy-start.3
  95.2 0.9 copy-done.3
  96.1 4.0 %factor.1 = (f32[1280,128]{1,0:T(8,128)S(1)}, f32[31,32,128]{2,1,0:T(8,128)S(1)}, f32[31,32,128]{2,1,0:T(8,128)S(1)}) custom-call(f32[256,128]{1,0:T(8,128)S(1)} %bitcast.23), custom_call_target="tpu_custom_call" | custom-call | tf_op jit(solution)/shard_map/factor/pallas_call | solution.py:319
  100.1 11.4 %first_ortho.1 = (f32[32,64,512]{2,1,0:T(8,128)S(1)}, f32[16,16,128]{2,1,0:T(8,128)S(1)}) custom-call(f32[4,2048,128]{2,1,0:T(8,128)} %get-tuple-element.12.spectrum, f32[1280,128]{1,0:T(8,128)S(1)} %get-tuple-element.14.inverse), custom_call_target="tpu_custom_call" | custom-call | tf_op jit(solution)/shard_map/first_ortho/pallas_call | solution.py:393
  111.5 0.0 copy-start
  111.5 1.9 %copy-done = f32[32,64,512]{2,1,0:T(8,128)} copy-done((f32[32,64,512]{2,1,0:T(8,128)}, f32[32,64,512]{2,1,0:T(8,128)S(1)}, u32[]{:S(2)}) %copy-start) | copy-done | bytes 4194328
  113.5 0.0 copy-start.5
  113.5 0.7 copy-done.5
  114.1 21.8 %global_sum.3 = f32[16,16,128]{2,1,0:T(8,128)} custom-call(f32[16,16,128]{2,1,0:T(8,128)} %copy-done.5), custom_call_target="tpu_custom_call" | custom-call | tf_op jit(solution)/shard_map/global_sum/pallas_call | solution.py:232
  136.0 0.0 copy-start.1
  136.0 0.0 copy-start.2
  136.0 1.0 copy-done.2
  137.0 5.8 %finish.1 = (f32[1280,128]{1,0:T(8,128)S(1)}, f32[31,32,128]{2,1,0:T(8,128)S(1)}, f32[31,32,128]{2,1,0:T(8,128)S(1)}) custom-call(f32[256,128]{1,0:T(8,128)S(1)} %bitcast.22, f32[31,32,128]{2,1,0:T(8,128)S(1)} %get-tuple-element.17.refs_1_, f32[31,32,128]{2,1,0:T(8,128)S(1)} %get-tuple-element.18.refs_2_), custom_call_target="tpu_custom_call" | custom-call | tf_op jit(solution)/shard_map/finish/pallas_call | solution.py:364
  142.8 0.1 slice_bitcast_fusion
  142.9 0.1 maximum_bitcast_fusion
  143.0 1.7 %copy.7 = f32[2,33,31,31]{1,0,3,2:T(2,128)} copy(f32[2,33,31,31]{1,3,2,0:T(8,128)S(1)} %maximum_bitcast_fusion) | data formatting | bytes 507408
  144.7 0.0 copy-done.1
  144.7 2.7 %modes.1 = f32[33,248,128]{2,1,0:T(8,128)} custom-call(f32[32,64,512]{2,1,0:T(8,128)S(1)} %copy-done.1, f32[1280,128]{1,0:T(8,128)S(1)} %get-tuple-element.19.inverse), custom_call_target="tpu_custom_call" | custom-call | tf_op jit(solution)/shard_map/modes/pallas_call | solution.py:443
Async XLA Ops:
  0.6 62.6 %copy-start.6 = (bf16[64,384]{1,0:T(8,128)(2,1)S(1)}, bf16[64,384]{1,0:T(8,128)(2,1)}, u32[]{:S(2)}) copy-start(bf16[64,384]{1,0:T(8,128)(2,1)} %constant.2.clone.table) | copy-start | bytes 147460
  0.6 62.6 %copy-start.7 = (f32[512]{0:T(512)S(1)}, f32[512]{0:T(512)}, u32[]{:S(2)}) copy-start(f32[512]{0:T(512)} %param.4) | copy-start | bytes 6148
  71.4 0.7 copy-start.4
  95.2 0.9 copy-start.3
  111.5 2.0 %copy-start = (f32[32,64,512]{2,1,0:T(8,128)}, f32[32,64,512]{2,1,0:T(8,128)S(1)}, u32[]{:S(2)}) copy-start(f32[32,64,512]{2,1,0:T(8,128)S(1)} %get-tuple-element.15.ortho) | copy-start | bytes 12582916
  113.5 0.7 copy-start.5
  136.0 8.8 %copy-start.1 = (f32[32,64,512]{2,1,0:T(8,128)S(1)}, f32[32,64,512]{2,1,0:T(8,128)}, u32[]{:S(2)}) copy-start(f32[32,64,512]{2,1,0:T(8,128)} %copy-done) | copy-start | bytes 12582916
  136.0 1.1 copy-start.2
where the time goes:
time: 148 us
  Pallas kernels  77 us (52%)
  blocking collectives  60.8 us (41%)
  local copies, waits for them, and re-layouts  8.82 us (6%)
    all_to_all x1, blocking collectives, shards(): lax.all_to_all(snapshots, 'tm', split_axis=1, concat_axis=0, tiled=True)  60.8 us
    pallas_call x2, Pallas kernels, global_sum(): pl.pallas_call(sum_kernel, out_shape=jax.ShapeDtypeStruct(packed.shape, p...  45 us
    pallas_call x1, Pallas kernels, first_ortho(): pl.pallas_call(first_kernel, out_shape=(jax.ShapeDtypeStruct((SLOTS, SEG,...  11.4 us
    pallas_call x1, Pallas kernels, spectra(): pl.pallas_call(spectrum_kernel, out_shape=(jax.ShapeDtypeStruct((points /...  8.1 us
    unnamed x17, local copies, waits for them, and re-layouts  6.93 us
    pallas_call x1, Pallas kernels, finish(): pl.pallas_call(lambda *refs: finish_kernel(1.0 / points_total, *refs), ou...  5.78 us
    pallas_call x1, Pallas kernels, factor(): pl.pallas_call(lambda *refs: factor_kernel(1.0 / points_total, *refs), ou...  3.98 us

commit v1 on v0

v1 whole, which is shorter than its diff:
```python
import jax
import jax.numpy as jnp
import ml_dtypes
import numpy as np
from jax import lax
from jax.experimental import pallas as pl
from jax.experimental.pallas import tpu as pltpu
from jax.sharding import PartitionSpec as P

SEG = 64
HOP = 32
NF = 33
NT = 1024
NB = 31
MESH = pl.DeviceIdType.MESH

VMEM = pl.BlockSpec(memory_space=pltpu.VMEM)
TILE = 32
SLOTS = 32
LINES = SEG + 1
TILE_LINES = TILE + 1
SLOT_LINES = 41


def fourier_table():
    sample = np.arange(SEG)[:, None]
    column = np.arange(SEG)[None, :]
    frequency = np.where(column < NF, column, column - HOP)
    window = 0.5 - 0.5 * np.cos(2.0 * np.pi * sample / SEG)
    phase_angle = 2.0 * np.pi * ((frequency * sample) % SEG) / SEG
    waveform = np.where(column < NF, np.cos(phase_angle), -np.sin(phase_angle))
    return (waveform * window / np.sqrt(3 * SEG / 8)).astype(np.float32)


def table_parts():
    table = fourier_table().T
    high = table.astype(ml_dtypes.bfloat16)
    rest = table - high.astype(np.float32)
    middle = rest.astype(ml_dtypes.bfloat16)
    low = (rest - middle.astype(np.float32)).astype(ml_dtypes.bfloat16)
    return np.concatenate([high, high, middle, high, middle, low], axis=1)


def parts_of(value, count):
    parts = []
    for _ in range(count):
        part = value.astype(jnp.bfloat16)
        parts.append(part)
        value = value - part.astype(jnp.float32)
    return parts


def left6(value):
    high, middle, low = parts_of(value, 3)
    return jnp.concatenate([high, high, middle, high, middle, low], axis=1)


def right6(value):
    high, middle, low = parts_of(value, 3)
    return jnp.concatenate([high, middle, high, low, middle, high], axis=0)


def left3(value):
    high, low = parts_of(value, 2)
    return jnp.concatenate([high, high, low], axis=1)


def right3(value):
    high, low = parts_of(value, 2)
    return jnp.concatenate([high, low, high], axis=0)


def multiply(left, right):
    return jnp.dot(left, right, preferred_element_type=jnp.float32)


def self_product(value, count):
    stacked = jnp.concatenate(parts_of(value, count), axis=0)
    whole = lax.dot_general(
        stacked, stacked, (((1,), (1,)), ((), ())), preferred_element_type=jnp.float32
    )
    size = value.shape[0]
    rows = sum(whole[i * size : (i + 1) * size] for i in reversed(range(count)))
    return sum(rows[:, i * size : (i + 1) * size] for i in reversed(range(count)))


def gram_tile(product, slot):
    top_left = product[:TILE, :TILE]
    bottom_right = product[TILE:, TILE:]
    row = lax.broadcasted_iota(jnp.int32, (TILE, TILE), 0)
    column = lax.broadcasted_iota(jnp.int32, (TILE, TILE), 1)
    if slot == 0:
        return jnp.where(column >= row, top_left, pltpu.roll(bottom_right, 1, 0))
    imaginary = product[:TILE, TILE:] - product[TILE:, :TILE]
    return jnp.where(column >= row, top_left + bottom_right, imaginary)


def put_tiles(out, group, tiles, add):
    joined = jnp.concatenate(tiles, axis=1)
    if add:
        joined = joined + jnp.concatenate([out[2 * group], out[2 * group + 1]], axis=0)
    out[2 * group] = joined[:16]
    out[2 * group + 1] = joined[16:]


def slot_rows(spectrum, slot, panels):
    halves = [
        [
            spectrum[panel, pl.ds(slot + half, TILE, stride=LINES), :]
            for panel in panels
        ]
        for half in (0, 32)
    ]
    return jnp.concatenate([jnp.concatenate(row, axis=1) for row in halves], axis=0)


PIECES = ((0, 384), (384, 128))


def spectrum_kernel(
    snapshots, weights, table, spectrum, result,
    first, second, packed, parts, root, send, recv, own, *sums,
):
    n = lax.axis_size("tm")
    pts = lax.axis_size("pts")
    me = lax.axis_index("tm")
    points = weights.shape[1]
    fetches = [
        pltpu.make_async_copy(table, parts, own.at[2]),
        pltpu.make_async_copy(weights, root, own.at[3]),
    ]
    for fetch in fetches:
        fetch.start()
    each(n, lambda d: greet(ahead("tm", d, n)))
    each(pts, lambda d: greet(ahead("pts", d, pts)))
    pl.semaphore_wait(pltpu.get_barrier_semaphore(), n + pts - 2)
    mine = pl.ds(pl.multiple_of(SEG * me, SEG), SEG)
    pieces = list(zip(range(2), PIECES, (first, second)))

    def column(device, start, width):
        return pl.ds(pl.multiple_of(device * points + start, 128), width)

    def travel(piece, d):
        index, (start, width), target = piece
        to = ahead("tm", d, n)
        return remote(
            snapshots.at[:, column(to["tm"], start, width)],
            target.at[mine, :],
            send.at[index, d],
            recv.at[index, d],
            to,
        )

    def stay(piece):
        index, (start, width), target = piece
        return pltpu.make_async_copy(
            snapshots.at[:, column(me, start, width)], target.at[mine, :], own.at[index]
        )

    for piece in pieces:
        each(n, lambda d: travel(piece, d).start())
        stay(piece).start()
    for fetch in fetches:
        fetch.wait()
    for panel in range(spectrum.shape[0]):
        spectrum[panel, NB * LINES :, :] = jnp.zeros((LINES, 128), jnp.float32)
    for piece in pieces:
        index, (start, width), target = piece
        stay(piece).wait()
        each(n, lambda d: travel(piece, d).wait_recv())
        panels = range(start // 128, (start + width) // 128)
        scale = jnp.sqrt(root[:, start : start + width])

        for b in range(NB):
            rows = target[HOP * b : HOP * b + SEG, :]
            value = multiply(parts[...], right6(rows)) * scale
            for panel in panels:
                at = 128 * panel - start
                spectrum[panel, LINES * b : LINES * b + SEG, :] = value[:, at : at + 128]
        for group in range(8):
            tiles = []
            for slot in range(group, SLOTS, 8):
                value = slot_rows(spectrum, slot, panels)
                tiles.append(gram_tile(self_product(value, 3), slot))
            put_tiles(packed, group, tiles, index > 0)
    for piece in pieces:
        each(n, lambda d: travel(piece, d).wait_send())
    sum_stages(packed, result, *sums)


def spectra(snapshots, weights):
    points = weights.shape[0]
    n = lax.axis_size("tm")
    dma = pltpu.SemaphoreType.DMA
    return pl.pallas_call(
        spectrum_kernel,
        out_shape=(
            jax.ShapeDtypeStruct((points // 128, TILE * LINES, 128), jnp.float32),
            jax.ShapeDtypeStruct(CHUNKS, jnp.float32),
        ),
        in_specs=[pl.BlockSpec(memory_space=pltpu.HBM)] * 3,
        out_specs=(VMEM, VMEM),
        scratch_shapes=[pltpu.VMEM((NT, width), jnp.float32) for _, width in PIECES]
        + [
            pltpu.VMEM(CHUNKS, jnp.float32),
            pltpu.VMEM((SEG, 6 * SEG), jnp.bfloat16),
            pltpu.VMEM((1, points), jnp.float32),
            dma((2, n)),
            dma((2, n)),
            dma((4,)),
        ]
        + sum_scratch(),
        compiler_params=pltpu.CompilerParams(
            vmem_limit_bytes=24 << 20, collective_id=0, has_side_effects=True
        ),
        name="spectra",
    )(*(pltpu.with_memory_space_constraint(x, pltpu.HBM) for x in (snapshots, weights.reshape(1, points), jnp.asarray(table_parts()))))


def remote(source, target, send, recv, device):
    return pltpu.make_async_remote_copy(
        src_ref=source, dst_ref=target, send_sem=send, recv_sem=recv,
        device_id=device, device_id_type=MESH,
    )


def each(count, action):
    def step(d, carry):
        action(d)
        return carry

    lax.fori_loop(1, count, step, 0)


def greet(device):
    pl.semaphore_signal(
        pltpu.get_barrier_semaphore(), inc=1, device_id=device, device_id_type=MESH
    )


def ahead(axis, d, n):
    return {axis: lax.rem(lax.axis_index(axis) + d, n)}


def sibling():
    me = lax.axis_index("tm")
    return {"tm": me + 1 - 2 * lax.rem(me, 2)}


def sum_stages(x_ref, o_ref, half, part, total, share, whole, full, *sems):
    send0, recv0, send1, recv1, send2, recv2, send3, recv3, send4, recv4 = sems
    me_p = lax.axis_index("pts")
    me_t = lax.axis_index("tm")
    core = lax.rem(me_t, 2)
    chip = me_t // 2
    n = part.shape[0]
    chips = share.shape[0]
    own_lines = pl.ds(pl.multiple_of(8 * core, 8), 8)
    other_lines = pl.ds(pl.multiple_of(8 - 8 * core, 8), 8)
    swap = remote(x_ref.at[:, other_lines, :], half, send0, recv0, sibling())

    def scatter(d):
        to = ahead("pts", d, n)
        return remote(full.at[to["pts"]], part.at[d], send1.at[d], recv1.at[d], to)

    def exchange(d):
        to = ahead("tm", 2 * d, 2 * chips)
        return remote(total, share.at[chip], send2.at[d], recv2.at[d], to)

    def gather(d):
        to = ahead("pts", d, n)
        return remote(whole, o_ref.at[me_p, own_lines, :], send3.at[d], recv3.at[d], to)

    back = remote(
        o_ref.at[:, own_lines, :], o_ref.at[:, own_lines, :], send4, recv4, sibling()
    )
    swap.start()
    swap.wait_recv()
    full[...] = x_ref[:, own_lines, :] + half[...]
    each(n, lambda d: scatter(d).start())
    part[0] = full[me_p]
    each(n, lambda d: scatter(d).wait_recv())
    total[...] = jnp.sum(part[...], axis=0)
    each(chips, lambda d: exchange(d).start())
    share[chip] = total[...]
    each(chips, lambda d: exchange(d).wait_recv())
    whole[...] = jnp.sum(share[...], axis=0)
    each(n, lambda d: gather(d).start())
    o_ref[me_p, own_lines, :] = whole[...]
    each(n, lambda d: gather(d).wait_recv())
    back.start()
    swap.wait_send()
    each(n, lambda d: scatter(d).wait_send())
    each(chips, lambda d: exchange(d).wait_send())
    each(n, lambda d: gather(d).wait_send())
    back.wait()


CHUNKS = (16, 16, 128)


def sum_scratch():
    n, lines, lanes = CHUNKS
    chips = lax.axis_size("tm") // 2
    dma = pltpu.SemaphoreType.DMA
    buffer = pltpu.VMEM((n, lines // 2, lanes), jnp.float32)
    return [
        buffer,
        buffer,
        pltpu.VMEM((lines // 2, lanes), jnp.float32),
        pltpu.VMEM((chips, lines // 2, lanes), jnp.float32),
        pltpu.VMEM((lines // 2, lanes), jnp.float32),
        buffer,
        dma, dma, dma((n,)), dma((n,)), dma((chips,)), dma((chips,)),
        dma((n,)), dma((n,)), dma, dma,
    ]


def factor_lanes(scale, packed, tiles, state_real, state_imag):
    column = lax.broadcasted_iota(jnp.int32, (TILE, 128), 0)
    lane = lax.broadcasted_iota(jnp.int32, (TILE, 128), 1)
    for b in range(TILE):
        lines = packed[pl.ds(b, 8, stride=TILE), :]
        spread = jnp.concatenate(
            [lines] + [pltpu.roll(lines, 128 - 32 * s, 1) for s in (1, 2, 3)]
            + [jnp.zeros((96, 128), jnp.float32)],
            axis=0,
        )
        line = TILE_LINES * b
        tiles[line : line + TILE, :] = jnp.transpose(spread)[:TILE] * scale
    tiles[TILE * TILE_LINES :, :] = jnp.zeros((TILE, 128), jnp.float32)
    for b in range(NB):
        line = TILE_LINES * b
        straight = tiles[line : line + TILE, :]
        turned = tiles[pl.ds(b, TILE, stride=TILE_LINES), :]
        line = TILE_LINES * (b + 1)
        below = tiles[line : line + TILE, :]
        below_turned = tiles[pl.ds(TILE_LINES + b, TILE, stride=TILE_LINES), :]
        last = pltpu.roll(jnp.where(column <= b, below, below_turned), 32, 1)
        real = jnp.where(column >= b, straight, turned)
        real = jnp.where(lane == 32, last, real)
        imag = jnp.where(column < b, straight, -turned)
        state_real[b] = jnp.where(lane > 32, jnp.where(column == b, 1.0, 0.0), real)
        state_imag[b] = jnp.where(
            (lane == 0) | (lane >= 32) | (column == b), 0.0, imag
        )
    for k in range(NB):
        here = column == k
        inverse = 1.0 / jnp.sqrt(state_real[k, k : k + 1, :])
        row_real = jnp.where(here, inverse, state_real[k] * inverse)
        row_imag = jnp.where(here, 0.0, state_imag[k] * inverse)
        state_real[k] = row_real
        state_imag[k] = row_imag

        def eliminate(i, carry):
            pick_real = state_real[k, pl.ds(i, 1), :]
            pick_imag = state_imag[k, pl.ds(i, 1), :]
            work_real = jnp.where(here, 0.0, state_real[i])
            work_imag = jnp.where(here, 0.0, state_imag[i])
            state_real[i] = work_real - (pick_real * row_real + pick_imag * row_imag)
            state_imag[i] = work_imag - (pick_real * row_imag - pick_imag * row_real)
            return carry

        lax.fori_loop(k + 1, NB, eliminate, 0, unroll=True)


def write_inverse(state_real, state_imag, inverse):
    column = lax.broadcasted_iota(jnp.int32, (TILE, 128), 0)
    lane = lax.broadcasted_iota(jnp.int32, (TILE, 128), 1)
    for k in range(NB):
        keep = column <= k
        real = jnp.where(keep, state_real[k], 0.0)
        imag = jnp.where(keep, state_imag[k], 0.0)
        lower = jnp.where(lane == 0, pltpu.roll(real, 96, 1), real)
        joined = jnp.concatenate([real, imag, -imag, lower], axis=0)
        line = SLOT_LINES * k
        inverse[line : line + SLOTS, :] = jnp.transpose(joined)[:SLOTS]
    line = SLOT_LINES * NB
    inverse[line : line + SLOTS, :] = jnp.zeros((SLOTS, 128), jnp.float32)


def factor_kernel(scale, packed, inverse, state_real, state_imag, tiles):
    factor_lanes(scale, packed, tiles, state_real, state_imag)
    write_inverse(state_real, state_imag, inverse)


TILES = pltpu.VMEM((TILE * TILE_LINES + TILE, 128), jnp.float32)
STATE = jax.ShapeDtypeStruct((NB, TILE, 128), jnp.float32)
INVERSE = jax.ShapeDtypeStruct((TILE * SLOT_LINES, 128), jnp.float32)


def factor(packed, points_total):
    return pl.pallas_call(
        lambda *refs: factor_kernel(1.0 / points_total, *refs),
        out_shape=(INVERSE, STATE, STATE),
        in_specs=[VMEM],
        out_specs=(VMEM,) * 3,
        scratch_shapes=[TILES],
        compiler_params=pltpu.CompilerParams(vmem_limit_bytes=24 << 20),
        name="factor",
    )(packed.reshape(256, 128))


def slot_matrix(inverse, slot):
    lines = inverse[pl.ds(slot, TILE, stride=SLOT_LINES), :]
    return jnp.concatenate([lines[:, :64], lines[:, 64:]], axis=0)


def first_kernel(spectrum, inverse, ortho, result, packed, *sums):
    pts = lax.axis_size("pts")
    chips = lax.axis_size("tm") // 2
    greet(sibling())
    each(pts, lambda d: greet(ahead("pts", d, pts)))
    each(chips, lambda d: greet(ahead("tm", 2 * d, 2 * chips)))
    for slot in range(SLOTS):
        value = slot_rows(spectrum, slot, range(spectrum.shape[0]))
        ortho[slot] = multiply(left6(slot_matrix(inverse, slot)), right6(value))
    for group in range(8):
        tiles = [
            gram_tile(self_product(ortho[slot], 2), slot)
            for slot in range(group, SLOTS, 8)
        ]
        put_tiles(packed, group, tiles, False)
    pl.semaphore_wait(pltpu.get_barrier_semaphore(), pts + chips - 1)
    sum_stages(packed, result, *sums)


def first_ortho(spectrum, inverse):
    points = spectrum.shape[0] * 128
    return pl.pallas_call(
        first_kernel,
        out_shape=(
            jax.ShapeDtypeStruct((SLOTS, SEG, points), jnp.float32),
            jax.ShapeDtypeStruct(CHUNKS, jnp.float32),
        ),
        in_specs=[VMEM] * 2,
        out_specs=(VMEM, VMEM),
        scratch_shapes=[pltpu.VMEM(CHUNKS, jnp.float32)] + sum_scratch(),
        compiler_params=pltpu.CompilerParams(
            vmem_limit_bytes=24 << 20, collective_id=1, has_side_effects=True
        ),
        name="first_ortho",
    )(spectrum, inverse)


def send_modes(ortho, inverse, modes, held, sems):
    copies = []
    panels = ortho.shape[2] // 128
    step = 2 * panels

    def put(frequency, part, value):
        for panel in range(panels):
            held[frequency, pl.ds(2 * panel + part, NB, stride=step), :] = value[
                :NB, 128 * panel : 128 * (panel + 1)
            ]

    def send(frequency):
        copy = pltpu.make_async_copy(
            held.at[frequency], modes.at[frequency], sems.at[frequency]
        )
        copy.start()
        copies.append(copy)

    for slot in range(SLOTS):
        value = multiply(left3(slot_matrix(inverse, slot)), right3(ortho[slot]))
        put(slot, 0, value[:TILE])
        if slot:
            put(slot, 1, value[TILE:])
        else:
            nothing = jnp.zeros((TILE, value.shape[1]), jnp.float32)
            put(0, 1, nothing)
            put(NF - 1, 0, value[TILE:])
            put(NF - 1, 1, nothing)
            send(NF - 1)
        send(slot)
    return copies


def finish_kernel(
    scale, packed, ortho, first_real, first_imag, modes, triangle,
    held, sems, inverse, tiles, state_real, state_imag, right_real, right_imag,
):
    factor_lanes(scale, packed, tiles, state_real, state_imag)
    write_inverse(state_real, state_imag, inverse)
    copies = send_modes(ortho, inverse, modes, held, sems)
    column = lax.broadcasted_iota(jnp.int32, (TILE, 128), 0)
    for k in range(NB):
        real = first_real[k]
        diagonal = jnp.where(column == k, 1.0 / real, 0.0)
        right_real[k] = jnp.where(column > k, real, diagonal)
        right_imag[k] = jnp.where(column > k, first_imag[k], 0.0)
    for i in range(NB):
        own = 1.0 / state_real[i, i : i + 1, :]
        start = (own * right_real[i], own * right_imag[i])

        def gather(k, total):
            total_real, total_imag = total
            pick_real = state_real[i, pl.ds(k, 1), :]
            pick_imag = state_imag[i, pl.ds(k, 1), :]
            row_real = right_real[k]
            row_imag = right_imag[k]
            return (
                total_real + (pick_real * row_real - pick_imag * row_imag),
                total_imag + (pick_real * row_imag + pick_imag * row_real),
            )

        total = lax.fori_loop(i + 1, NB, gather, start, unroll=True)
        for part in range(2):
            triangle[i, pl.ds(part, NB, stride=2), :] = total[part][:NB]
    for copy in copies:
        copy.wait()


def finish(packed, ortho, first_real, first_imag, points_total):
    points = ortho.shape[2]
    shape = (NF, NB * points // 64, 128)
    modes, triangle = pl.pallas_call(
        lambda *refs: finish_kernel(1.0 / points_total, *refs),
        out_shape=(
            jax.ShapeDtypeStruct(shape, jnp.float32),
            jax.ShapeDtypeStruct((NB, 2 * NB, 128), jnp.float32),
        ),
        in_specs=[VMEM] * 4,
        out_specs=(pl.BlockSpec(memory_space=pl.ANY), VMEM),
        scratch_shapes=[
            pltpu.VMEM(shape, jnp.float32),
            pltpu.SemaphoreType.DMA((NF,)),
            pltpu.VMEM(INVERSE.shape, jnp.float32),
            TILES,
        ]
        + [pltpu.VMEM(STATE.shape, jnp.float32)] * 4,
        compiler_params=pltpu.CompilerParams(vmem_limit_bytes=24 << 20),
        name="finish",
    )(packed.reshape(256, 128), ortho, first_real, first_imag)
    modes = modes.reshape(NF, NB, points // 128, 2, 128)
    modes = jnp.transpose(modes, (3, 0, 1, 2, 4)).reshape(2, NF, NB, points)
    triangle = triangle.reshape(NB, NB, 2, 128)[..., :NF]
    return modes, jnp.transpose(triangle, (2, 3, 0, 1))


def shards(snapshots, weights):
    points_total = weights.shape[0] * lax.axis_size("tm") * lax.axis_size("pts")
    spectrum, packed = spectra(snapshots, weights)
    inverse, first_real, first_imag = factor(packed, points_total)
    ortho, packed = first_ortho(spectrum, inverse)
    return finish(packed, ortho, first_real, first_imag, points_total)


def solution(mesh):
    placed = (P("tm", "pts"), P(("pts", "tm")))
    return jax.shard_map(
        shards,
        mesh=mesh,
        in_specs=placed,
        out_specs=(P(None, None, None, ("pts", "tm")), P()),
        check_vma=False,
    )
```

time: 148 us -> 116 us (0.78)
  blocking collectives: 60.8 us -> 0 us
  Pallas kernels: 77 us -> 114 us
  local copies, waits for them, and re-layouts: 8.82 us -> 1.62 us
    pallas_call x1, Pallas kernels: 8.1 us -> 77.9 us  [spectra(): pl.pallas_call(spectrum_kernel, out_shape=(jax.ShapeDtypeStruct((points /...]
    all_to_all x1 -> x0, blocking collectives: 60.8 us -> none  [shards(): lax.all_to_all(snapshots, 'tm', split_axis=1, concat_axis=0, tiled=True)]
    pallas_call x3 -> x0, Pallas kernels: 47.7 us -> none  [the longest x2 45 us: global_sum(): pl.pallas_call(sum_kernel, out_shape=jax.ShapeDtypeStruct(packed.shape, p...]
    pallas_call x1, Pallas kernels: 11.4 us -> 23.7 us  [first_ortho(): pl.pallas_call(first_kernel, out_shape=(jax.ShapeDtypeStruct((SLOTS, SEG,...]
    unnamed x17 -> x0, local copies, waits for them, and re-layouts: 6.93 us -> none
    pallas_call x1, Pallas kernels: 5.78 us -> 8.51 us  [finish(): pl.pallas_call(lambda *refs: finish_kernel(1.0 / points_total, *refs), ou...]
    all_to_all x1 -> x0, local copies, waits for them, and re-layouts: 1.81 us -> none  [shards(): lax.all_to_all(snapshots, 'tm', split_axis=1, concat_axis=0, tiled=True)]
where the time goes in v1:
time: 116 us
  Pallas kernels  114 us (98%)
  local copies, waits for them, and re-layouts  1.62 us (1%)
    pallas_call x1, Pallas kernels, spectra(): pl.pallas_call(spectrum_kernel, out_shape=(jax.ShapeDtypeStruct((points /...  77.9 us
    pallas_call x1, Pallas kernels, first_ortho(): pl.pallas_call(first_kernel, out_shape=(jax.ShapeDtypeStruct((SLOTS, SEG,...  23.7 us
    pallas_call x1, Pallas kernels, finish(): pl.pallas_call(lambda *refs: finish_kernel(1.0 / points_total, *refs), ou...  8.51 us
    pallas_call x1, Pallas kernels, factor(): pl.pallas_call(lambda *refs: factor_kernel(1.0 / points_total, *refs), ou...  3.65 us

profile of v1, /device:TPU:1, one launch (start us, length us, event | category | flops | bytes accessed | tf_op | source)
XLA Modules:
  0.0 116.1 jit_solution(18277870860688857621)
XLA Ops:
  0.6 77.9 %spectra.1 = (f32[4,2080,128]{2,1,0:T(8,128)S(1)}, f32[16,16,128]{2,1,0:T(8,128)S(1)}) custom-call(f32[64,8192]{1,0:T(8,128)} %snapshots.1, f32[1,512]{1,0:T(1,128)} %bitcast.12, bf16[64,384]{1,0:T(8,128)(2,1)} %constant.2.clone.table), custom_call_target="tpu_custom_call" | custom-call | tf_op jit(solution)/shard_map/spectra/pallas_call | solution.py:195
  78.6 3.7 %factor.1 = (f32[1312,128]{1,0:T(8,128)S(1)}, f32[31,32,128]{2,1,0:T(8,128)S(1)}, f32[31,32,128]{2,1,0:T(8,128)S(1)}) custom-call(f32[256,128]{1,0:T(8,128)S(1)} %bitcast.10), custom_call_target="tpu_custom_call" | custom-call | tf_op jit(solution)/shard_map/factor/pallas_call | solution.py:393
  82.2 23.7 %first_ortho.1 = (f32[32,64,512]{2,1,0:T(8,128)S(1)}, f32[16,16,128]{2,1,0:T(8,128)S(1)}) custom-call(f32[4,2080,128]{2,1,0:T(8,128)S(1)} %get-tuple-element.11.spectrum, f32[1312,128]{1,0:T(8,128)S(1)} %get-tuple-element.13.inverse), custom_call_target="tpu_custom_call" | custom-call | tf_op jit(solution)/shard_map/first_ortho/pallas_call | solution.py:430
  106.0 8.5 %finish.1 = (f32[33,248,128]{2,1,0:T(8,128)}, f32[31,62,128]{2,1,0:T(8,128)S(1)}) custom-call(f32[256,128]{1,0:T(8,128)S(1)} %bitcast.11, f32[32,64,512]{2,1,0:T(8,128)S(1)} %get-tuple-element.15.refs_1_, f32[31,32,128]{2,1,0:T(8,128)S(1)} %get-tuple-element.16.refs_2_, f32[31,32,128]{2,1,0:T(8,128)S(1)} %get-tuple-element.17.refs_3_), custom_call_target="tpu_custom_call" | custom-call | tf_op jit(solution)/shard_map/finish/pallas_call | solution.py:517
  114.5 0.6 reshape.27
  115.1 1.0 slice_bitcast_fusion

commit v2 on v1

v2 whole, which is shorter than its diff:
```python
import math

import jax
import jax.numpy as jnp
import ml_dtypes
import numpy as np
from jax import lax
from jax.experimental import pallas as pl
from jax.experimental.pallas import tpu as pltpu
from jax.sharding import PartitionSpec as P

SEG = 64
HOP = 32
NF = 33
NT = 1024
NB = 31
MESH = pl.DeviceIdType.MESH

VMEM = pl.BlockSpec(memory_space=pltpu.VMEM)
TILE = 32
SLOTS = 32
LINES = SEG + 1
TILE_LINES = TILE + 1
SLOT_LINES = 41


def fourier_table():
    sample = np.arange(SEG)[:, None]
    column = np.arange(SEG)[None, :]
    frequency = np.where(column < NF, column, column - HOP)
    window = 0.5 - 0.5 * np.cos(2.0 * np.pi * sample / SEG)
    phase_angle = 2.0 * np.pi * ((frequency * sample) % SEG) / SEG
    waveform = np.where(column < NF, np.cos(phase_angle), -np.sin(phase_angle))
    return (waveform * window / np.sqrt(3 * SEG / 8)).astype(np.float32)


def table_parts():
    table = fourier_table().T
    high = table.astype(ml_dtypes.bfloat16)
    rest = table - high.astype(np.float32)
    middle = rest.astype(ml_dtypes.bfloat16)
    low = (rest - middle.astype(np.float32)).astype(ml_dtypes.bfloat16)
    return np.concatenate([high, high, middle, high, middle, low], axis=1)


def parts_of(value, count):
    parts = []
    for _ in range(count):
        part = value.astype(jnp.bfloat16)
        parts.append(part)
        value = value - part.astype(jnp.float32)
    return parts


def left6(value):
    high, middle, low = parts_of(value, 3)
    return jnp.concatenate([high, high, middle, high, middle, low], axis=1)


def right6(value):
    high, middle, low = parts_of(value, 3)
    return jnp.concatenate([high, middle, high, low, middle, high], axis=0)


def left3(value):
    high, low = parts_of(value, 2)
    return jnp.concatenate([high, high, low], axis=1)


def right3(value):
    high, low = parts_of(value, 2)
    return jnp.concatenate([high, low, high], axis=0)


def multiply(left, right):
    return jnp.dot(left, right, preferred_element_type=jnp.float32)


def self_product(value, count):
    stacked = jnp.concatenate(parts_of(value, count), axis=0)
    whole = lax.dot_general(
        stacked, stacked, (((1,), (1,)), ((), ())), preferred_element_type=jnp.float32
    )
    size = value.shape[0]
    rows = sum(whole[i * size : (i + 1) * size] for i in reversed(range(count)))
    return sum(rows[:, i * size : (i + 1) * size] for i in reversed(range(count)))


def gram_tile(product, slot):
    top_left = product[:TILE, :TILE]
    bottom_right = product[TILE:, TILE:]
    row = lax.broadcasted_iota(jnp.int32, (TILE, TILE), 0)
    column = lax.broadcasted_iota(jnp.int32, (TILE, TILE), 1)
    if slot == 0:
        return jnp.where(column >= row, top_left, pltpu.roll(bottom_right, 1, 0))
    imaginary = product[:TILE, TILE:] - product[TILE:, :TILE]
    return jnp.where(column >= row, top_left + bottom_right, imaginary)


def put_tiles(out, group, tiles, add):
    joined = jnp.concatenate(tiles, axis=1)
    if add:
        joined = joined + jnp.concatenate([out[2 * group], out[2 * group + 1]], axis=0)
    out[2 * group] = joined[:16]
    out[2 * group + 1] = joined[16:]


def slot_rows(spectrum, slot, panels):
    halves = [
        [
            spectrum[panel, pl.ds(slot + half, TILE, stride=LINES), :]
            for panel in panels
        ]
        for half in (0, 32)
    ]
    return jnp.concatenate([jnp.concatenate(row, axis=1) for row in halves], axis=0)


def remote(source, target, send, recv, device):
    return pltpu.make_async_remote_copy(
        src_ref=source, dst_ref=target, send_sem=send, recv_sem=recv,
        device_id=device, device_id_type=MESH,
    )


def greet(device):
    pl.semaphore_signal(
        pltpu.get_barrier_semaphore(), inc=1, device_id=device, device_id_type=MESH
    )


def ring_offsets(n):
    return sorted(range(1, n), key=lambda d: -min(d, n - d))


def square_offsets(n):
    side = math.isqrt(n)
    offsets = [(i, j) for i in range(side) for j in range(side) if i or j]
    return sorted(
        offsets, key=lambda o: -(min(o[0], side - o[0]) + min(o[1], side - o[1]))
    )


def sum_stages(x_ref, o_ref, part, total, share, whole, *sems):
    send1, recv1, send2, recv2, send3, recv3 = sems
    me_p = lax.axis_index("pts")
    me_t = lax.axis_index("tm")
    core = lax.rem(me_t, 2)
    chip = me_t // 2
    n = part.shape[0] // 2
    side = math.isqrt(n)
    chips = share.shape[0]

    def lines(k):
        return pl.ds(pl.multiple_of(8 * k, 8), 8)

    own_lines = pl.ds(pl.multiple_of(16 * me_p + 8 * core, 8), 8)
    peers = [(i, j, c) for i, j in square_offsets(n) for c in (0, 1)] + [(0, 0, 1)]

    def peer(offset):
        i, j, c = offset
        row = lax.rem(me_p // side + i, side)
        to_p = row * side + lax.rem(lax.rem(me_p, side) + j, side)
        to_core = lax.rem(core + c, 2)
        device = {"pts": to_p, "tm": me_t - core + to_core}
        return device, to_p, to_core, (i * side + j) * 2 + c

    def scatter(offset):
        device, to_p, to_core, slot = peer(offset)
        return remote(
            x_ref.at[to_p, lines(to_core), :], part.at[slot],
            send1.at[slot], recv1.at[slot], device,
        )

    def exchange(d):
        to = {"tm": lax.rem(me_t + 2 * d, 2 * chips)}
        return remote(total, share.at[chip], send2.at[d], recv2.at[d], to)

    def gather(offset):
        device, _, _, slot = peer(offset)
        return remote(
            whole, o_ref.at[own_lines, :], send3.at[slot], recv3.at[slot], device
        )

    scatters = [scatter(offset) for offset in peers]
    exchanges = [exchange(d) for d in ring_offsets(chips)]
    gathers = [gather(offset) for offset in peers]
    for copy in scatters:
        copy.start()
    part[0] = x_ref[me_p, lines(core), :]
    for copy in scatters:
        copy.wait_recv()
    total[...] = jnp.sum(part[...], axis=0)
    for copy in exchanges:
        copy.start()
    share[chip] = total[...]
    for copy in exchanges:
        copy.wait_recv()
    whole[...] = jnp.sum(share[...], axis=0)
    for copy in gathers:
        copy.start()
    o_ref[own_lines, :] = whole[...]
    for copy in gathers:
        copy.wait_recv()
    for copy in scatters + exchanges + gathers:
        copy.wait_send()


def all_greetings():
    n = lax.axis_size("pts")
    side = math.isqrt(n)
    me_p = lax.axis_index("pts")
    me_t = lax.axis_index("tm")
    core = lax.rem(me_t, 2)
    chips = lax.axis_size("tm") // 2
    devices = [{"tm": lax.rem(me_t + 2 * d, 2 * chips)} for d in ring_offsets(chips)]
    for i, j in square_offsets(n):
        row = lax.rem(me_p // side + i, side)
        to_p = row * side + lax.rem(lax.rem(me_p, side) + j, side)
        devices.append({"pts": to_p})
        devices.append({"pts": to_p, "tm": me_t + 1 - 2 * core})
    devices.append({"tm": me_t + 1 - 2 * core})
    return devices


CHUNKS = (16, 16, 128)
SUMS = (256, 128)


def sum_scratch():
    n, lines, lanes = CHUNKS
    chips = lax.axis_size("tm") // 2
    dma = pltpu.SemaphoreType.DMA
    piece = (lines // 2, lanes)
    return [
        pltpu.VMEM((2 * n,) + piece, jnp.float32),
        pltpu.VMEM(piece, jnp.float32),
        pltpu.VMEM((chips,) + piece, jnp.float32),
        pltpu.VMEM(piece, jnp.float32),
        dma((2 * n,)), dma((2 * n,)), dma((chips,)), dma((chips,)),
        dma((2 * n,)), dma((2 * n,)),
    ]


def factor_lanes(scale, packed, tiles, state_real, state_imag):
    column = lax.broadcasted_iota(jnp.int32, (TILE, 128), 0)
    lane = lax.broadcasted_iota(jnp.int32, (TILE, 128), 1)
    for b in range(TILE):
        lines = packed[pl.ds(b, 8, stride=TILE), :]
        spread = jnp.concatenate(
            [lines] + [pltpu.roll(lines, 128 - 32 * s, 1) for s in (1, 2, 3)]
            + [jnp.zeros((96, 128), jnp.float32)],
            axis=0,
        )
        line = TILE_LINES * b
        tiles[line : line + TILE, :] = jnp.transpose(spread)[:TILE] * scale
    tiles[TILE * TILE_LINES :, :] = jnp.zeros((TILE, 128), jnp.float32)
    for b in range(NB):
        line = TILE_LINES * b
        straight = tiles[line : line + TILE, :]
        turned = tiles[pl.ds(b, TILE, stride=TILE_LINES), :]
        line = TILE_LINES * (b + 1)
        below = tiles[line : line + TILE, :]
        below_turned = tiles[pl.ds(TILE_LINES + b, TILE, stride=TILE_LINES), :]
        last = pltpu.roll(jnp.where(column <= b, below, below_turned), 32, 1)
        real = jnp.where(column >= b, straight, turned)
        real = jnp.where(lane == 32, last, real)
        imag = jnp.where(column < b, straight, -turned)
        state_real[b] = jnp.where(lane > 32, jnp.where(column == b, 1.0, 0.0), real)
        state_imag[b] = jnp.where(
            (lane == 0) | (lane >= 32) | (column == b), 0.0, imag
        )
    line = lax.broadcasted_iota(jnp.int32, (8, 128), 0)
    for k in range(NB):
        here = line == k % 8
        pivot = state_real[k, k : k + 1, :]
        inverse = lax.rsqrt(pivot)
        inverse = inverse * (1.5 - (0.5 * pivot * inverse) * inverse)
        rows = []
        for at in range(0, TILE, 8):
            group = slice(at, at + 8)
            real = state_real[k, group] * inverse
            imag = state_imag[k, group] * inverse
            if at == k // 8 * 8:
                real = jnp.where(here, inverse, real)
                imag = jnp.where(here, 0.0, imag)
            state_real[k, group] = real
            state_imag[k, group] = imag
            rows.append((real, imag))
        for i in range(k + 1, NB):
            pick_real = state_real[k, i : i + 1]
            pick_imag = state_imag[k, i : i + 1]
            for at in range(0, TILE, 8):
                if at > k and at + 7 < i:
                    continue
                group = slice(at, at + 8)
                real, imag = rows[at // 8]
                work_real = state_real[i, group]
                work_imag = state_imag[i, group]
                if at == k // 8 * 8:
                    work_real = jnp.where(here, 0.0, work_real)
                    work_imag = jnp.where(here, 0.0, work_imag)
                state_real[i, group] = work_real - (pick_real * real + pick_imag * imag)
                state_imag[i, group] = work_imag - (pick_real * imag - pick_imag * real)


def write_inverse(state_real, state_imag, inverse):
    column = lax.broadcasted_iota(jnp.int32, (TILE, 128), 0)
    lane = lax.broadcasted_iota(jnp.int32, (TILE, 128), 1)
    for k in range(NB):
        keep = column <= k
        real = jnp.where(keep, state_real[k], 0.0)
        imag = jnp.where(keep, state_imag[k], 0.0)
        lower = jnp.where(lane == 0, pltpu.roll(real, 96, 1), real)
        joined = jnp.concatenate([real, imag, -imag, lower], axis=0)
        line = SLOT_LINES * k
        inverse[line : line + SLOTS, :] = jnp.transpose(joined)[:SLOTS]
    line = SLOT_LINES * NB
    inverse[line : line + SLOTS, :] = jnp.zeros((SLOTS, 128), jnp.float32)


TILES = pltpu.VMEM((TILE * TILE_LINES + TILE, 128), jnp.float32)
STATE = jax.ShapeDtypeStruct((NB, TILE, 128), jnp.float32)
INVERSE = (TILE * SLOT_LINES, 128)


def slot_matrix(inverse, slot):
    lines = inverse[pl.ds(slot, TILE, stride=SLOT_LINES), :]
    return jnp.concatenate([lines[:, :64], lines[:, 64:]], axis=0)


PIECES = ((0, 384), (384, 128))


def first_kernel(
    points_total, snapshots, weights, table, ortho, result, state_real, state_imag,
    first, second, packed, parts, root, send, recv, own, spectrum, inverse, tiles, gathered,
    *sums,
):
    n = lax.axis_size("tm")
    me = lax.axis_index("tm")
    points = weights.shape[1]
    fetches = [
        pltpu.make_async_copy(table, parts, own.at[2]),
        pltpu.make_async_copy(weights, root, own.at[3]),
    ]
    for fetch in fetches:
        fetch.start()
    chips = n // 2
    core = lax.rem(me, 2)
    others = [(d, c) for d in ring_offsets(chips) for c in (0, 1)] + [(0, 1)]

    def other(offset):
        d, c = offset
        to = lax.rem(me - core + 2 * d, n) + lax.rem(core + c, 2)
        return to, 2 * d + c

    for d in ring_offsets(chips):
        greet({"tm": other((d, 1))[0]})
    devices = all_greetings()
    for device in devices:
        greet(device)
    greeted = len(devices) + chips - 1
    pl.semaphore_wait(pltpu.get_barrier_semaphore(), greeted)
    mine = pl.ds(pl.multiple_of(SEG * me, SEG), SEG)
    pieces = list(zip(range(2), PIECES, (first, second)))

    def column(device, start, width):
        return pl.ds(pl.multiple_of(device * points + start, 128), width)

    def travel(piece, offset):
        index, (start, width), target = piece
        to, slot = other(offset)
        return remote(
            snapshots.at[:, column(to, start, width)],
            target.at[mine, :],
            send.at[index, slot],
            recv.at[index, slot],
            {"tm": to},
        )

    def stay(piece):
        index, (start, width), target = piece
        return pltpu.make_async_copy(
            snapshots.at[:, column(me, start, width)], target.at[mine, :], own.at[index]
        )

    for piece in pieces:
        for offset in others:
            travel(piece, offset).start()
        stay(piece).start()
    for fetch in fetches:
        fetch.wait()
    for panel in range(spectrum.shape[0]):
        spectrum[panel, NB * LINES :, :] = jnp.zeros((LINES, 128), jnp.float32)
    for piece in pieces:
        index, (start, width), target = piece
        stay(piece).wait()
        for offset in others:
            travel(piece, offset).wait_recv()
        panels = range(start // 128, (start + width) // 128)
        scale = jnp.sqrt(root[:, start : start + width])

        for b in range(NB):
            rows = target[HOP * b : HOP * b + SEG, :]
            value = multiply(parts[...], right6(rows)) * scale
            for panel in panels:
                at = 128 * panel - start
                spectrum[panel, LINES * b : LINES * b + SEG, :] = value[:, at : at + 128]
        for group in range(8):
            products = [
                gram_tile(self_product(slot_rows(spectrum, slot, panels), 3), slot)
                for slot in range(group, SLOTS, 8)
            ]
            put_tiles(packed, group, products, index > 0)
    half = len(sums) // 2
    sum_stages(packed, gathered, *sums[:half])
    factor_lanes(1.0 / points_total, gathered, tiles, state_real, state_imag)
    write_inverse(state_real, state_imag, inverse)
    for slot in range(SLOTS):
        value = slot_rows(spectrum, slot, range(spectrum.shape[0]))
        ortho[slot] = multiply(left6(slot_matrix(inverse, slot)), right6(value))
    for group in range(8):
        products = [
            gram_tile(self_product(ortho[slot], 2), slot)
            for slot in range(group, SLOTS, 8)
        ]
        put_tiles(packed, group, products, False)
    sum_stages(packed, result, *sums[half:])
    for piece in pieces:
        for offset in others:
            travel(piece, offset).wait_send()


def first_pass(snapshots, weights, points_total):
    points = weights.shape[0]
    n = lax.axis_size("tm")
    dma = pltpu.SemaphoreType.DMA
    inputs = (snapshots, weights.reshape(1, points), jnp.asarray(table_parts()))
    return pl.pallas_call(
        lambda *refs: first_kernel(points_total, *refs),
        out_shape=(
            jax.ShapeDtypeStruct((SLOTS, SEG, points), jnp.float32),
            jax.ShapeDtypeStruct(SUMS, jnp.float32),
            STATE,
            STATE,
        ),
        in_specs=[pl.BlockSpec(memory_space=pltpu.HBM)] * 3,
        out_specs=(VMEM,) * 4,
        scratch_shapes=[pltpu.VMEM((NT, width), jnp.float32) for _, width in PIECES]
        + [
            pltpu.VMEM(CHUNKS, jnp.float32),
            pltpu.VMEM((SEG, 6 * SEG), jnp.bfloat16),
            pltpu.VMEM((1, points), jnp.float32),
            dma((2, n)),
            dma((2, n)),
            dma((4,)),
            pltpu.VMEM((points // 128, TILE * LINES, 128), jnp.float32),
            pltpu.VMEM(INVERSE, jnp.float32),
            TILES,
            pltpu.VMEM(SUMS, jnp.float32),
        ]
        + sum_scratch() * 2,
        compiler_params=pltpu.CompilerParams(
            vmem_limit_bytes=32 << 20, collective_id=0, has_side_effects=True
        ),
        name="first_pass",
    )(*(pltpu.with_memory_space_constraint(x, pltpu.HBM) for x in inputs))


def send_modes(ortho, inverse, modes, held, sems):
    copies = []
    panels = ortho.shape[2] // 128
    step = 2 * panels

    def put(frequency, part, value):
        for panel in range(panels):
            held[frequency, pl.ds(2 * panel + part, NB, stride=step), :] = value[
                :NB, 128 * panel : 128 * (panel + 1)
            ]

    def send(frequency):
        copy = pltpu.make_async_copy(
            held.at[frequency], modes.at[frequency], sems.at[frequency]
        )
        copy.start()
        copies.append(copy)

    for slot in range(SLOTS):
        value = multiply(left3(slot_matrix(inverse, slot)), right3(ortho[slot]))
        put(slot, 0, value[:TILE])
        if slot:
            put(slot, 1, value[TILE:])
        else:
            nothing = jnp.zeros((TILE, value.shape[1]), jnp.float32)
            put(0, 1, nothing)
            put(NF - 1, 0, value[TILE:])
            put(NF - 1, 1, nothing)
            send(NF - 1)
        send(slot)
    return copies


def finish_kernel(
    scale, packed, ortho, first_real, first_imag, modes, triangle,
    held, sems, inverse, tiles, state_real, state_imag, right_real, right_imag, rows, row_sems,
):
    factor_lanes(scale, packed, tiles, state_real, state_imag)
    write_inverse(state_real, state_imag, inverse)
    copies = send_modes(ortho, inverse, modes, held, sems)
    column = lax.broadcasted_iota(jnp.int32, (TILE, 128), 0)
    for k in range(NB):
        real = first_real[k]
        diagonal = jnp.where(column == k, 1.0 / real, 0.0)
        right_real[k] = jnp.where(column > k, real, diagonal)
        right_imag[k] = jnp.where(column > k, first_imag[k], 0.0)
    for i in range(NB):
        first = i // 8 * 8
        own = 1.0 / state_real[i, i : i + 1, :]
        groups = range(first, TILE, 8)
        total_real = {at: own * right_real[i, at : at + 8] for at in groups}
        total_imag = {at: own * right_imag[i, at : at + 8] for at in groups}
        for k in range(i + 1, NB):
            pick_real = state_real[i, k : k + 1]
            pick_imag = state_imag[i, k : k + 1]
            for at in range(k // 8 * 8, TILE, 8):
                real = right_real[k, at : at + 8]
                imag = right_imag[k, at : at + 8]
                total_real[at] = total_real[at] + (pick_real * real - pick_imag * imag)
                total_imag[at] = total_imag[at] + (pick_real * imag + pick_imag * real)
        for part, total in enumerate((total_real, total_imag)):
            zeros = [jnp.zeros((8, 128), jnp.float32)] * (first // 8)
            line = jnp.concatenate(zeros + [total[at] for at in groups], axis=0)
            rows[i, :, part, :] = line[:NB, :NF]
        copy = pltpu.make_async_copy(rows.at[i], triangle.at[i], row_sems.at[i])
        copy.start()
        copies.append(copy)
    for copy in copies:
        copy.wait()


def finish(packed, ortho, first_real, first_imag, points_total):
    points = ortho.shape[2]
    shape = (NF, NB * points // 64, 128)
    modes, triangle = pl.pallas_call(
        lambda *refs: finish_kernel(1.0 / points_total, *refs),
        out_shape=(
            jax.ShapeDtypeStruct(shape, jnp.float32),
            jax.ShapeDtypeStruct((NB, NB, 2, NF), jnp.float32),
        ),
        in_specs=[VMEM] * 4,
        out_specs=(pl.BlockSpec(memory_space=pl.ANY),) * 2,
        scratch_shapes=[
            pltpu.VMEM(shape, jnp.float32),
            pltpu.SemaphoreType.DMA((NF,)),
            pltpu.VMEM(INVERSE, jnp.float32),
            TILES,
        ]
        + [pltpu.VMEM(STATE.shape, jnp.float32)] * 4
        + [
            pltpu.VMEM((NB, NB, 2, NF), jnp.float32),
            pltpu.SemaphoreType.DMA((NB,)),
        ],
        compiler_params=pltpu.CompilerParams(vmem_limit_bytes=24 << 20),
        name="finish",
    )(packed, ortho, first_real, first_imag)
    modes = modes.reshape(NF, NB, points // 128, 2, 128)
    modes = jnp.transpose(modes, (3, 0, 1, 2, 4)).reshape(2, NF, NB, points)
    return modes, jnp.transpose(triangle, (2, 3, 0, 1))


def shards(snapshots, weights):
    points_total = weights.shape[0] * lax.axis_size("tm") * lax.axis_size("pts")
    ortho, packed, *first = first_pass(snapshots, weights, points_total)
    return finish(packed, ortho, *first, points_total)


def solution(mesh):
    placed = (P("tm", "pts"), P(("pts", "tm")))
    return jax.shard_map(
        shards,
        mesh=mesh,
        in_specs=placed,
        out_specs=(P(None, None, None, ("pts", "tm")), P()),
        check_vma=False,
    )
```

time: 116 us -> 110 us (0.948)
  Pallas kernels: 114 us -> 109 us
  local copies, waits for them, and re-layouts: 1.62 us -> 0 us
    pallas_call x3 -> x1, Pallas kernels: 105 us -> 100 us  [first_pass(): pl.pallas_call(lambda *refs: first_kernel(points_total, *refs), out_shape...]
where the time goes in v2:
time: 110 us
  Pallas kernels  109 us (99%)
    pallas_call x1, Pallas kernels, first_pass(): pl.pallas_call(lambda *refs: first_kernel(points_total, *refs), out_shape...  100 us
    pallas_call x1, Pallas kernels, finish(): pl.pallas_call(lambda *refs: finish_kernel(1.0 / points_total, *refs), ou...  8.94 us

profile of v2, /device:TPU:1, one launch (start us, length us, event | category | flops | bytes accessed | tf_op | source)
XLA Modules:
  0.0 110.1 jit_solution(15080470729141420907)
XLA Ops:
  0.6 100.3 %first_pass.1 = (f32[32,64,512]{2,1,0:T(8,128)S(1)}, f32[256,128]{1,0:T(8,128)S(1)}, f32[31,32,128]{2,1,0:T(8,128)S(1)}, f32[31,32,128]{2,1,0:T(8,128)S(1)}) custom-call(f32[64,8192]{1,0:T(8,128)} %refs_0_.1, f32[1,512]{1,0:T(1,128)} %bitcast.7, bf16[64,384]{1,0:T(8,128)(2,1)} %constant.2.clone.refs_2_), custom_call_target="tpu_custom_call" | custom-call | tf_op jit(solution)/shard_map/first_pass/pallas_call | solution.py:440
  101.0 8.9 %finish.1 = (f32[33,248,128]{2,1,0:T(8,128)}, f32[31,31,2,33]{3,2,1,0:T(2,128)}) custom-call(f32[256,128]{1,0:T(8,128)S(1)} %get-tuple-element.8.refs_0_, f32[32,64,512]{2,1,0:T(8,128)S(1)} %get-tuple-element.9.refs_1_, f32[31,32,128]{2,1,0:T(8,128)S(1)} %get-tuple-element.10.refs_2_, f32[31,32,128]{2,1,0:T(8,128)S(1)} %get-tuple-element.11.refs_3_), custom_call_target="tpu_custom_call" | custom-call | tf_op jit(solution)/shard_map/finish/pallas_call | solution.py:545

commit v3 on v2

--- a/solution.py
+++ b/solution.py
@@ -123,6 +123,11 @@
     )
 
 
+def all_of(ref, send, recv):
+    me = lax.axis_index("tm")
+    return remote(ref, ref, send, recv, {"tm": me + 1 - 2 * lax.rem(me, 2)})
+
+
 def greet(device):
     pl.semaphore_signal(
         pltpu.get_barrier_semaphore(), inc=1, device_id=device, device_id_type=MESH
@@ -168,42 +173,37 @@
     def scatter(offset):
         device, to_p, to_core, slot = peer(offset)
         return remote(
-            x_ref.at[to_p, lines(to_core), :], part.at[slot],
-            send1.at[slot], recv1.at[slot], device,
+            x_ref.at[to_p, lines(to_core), :], part.at[slot], send1, recv1, device,
         )
 
     def exchange(d):
         to = {"tm": lax.rem(me_t + 2 * d, 2 * chips)}
-        return remote(total, share.at[chip], send2.at[d], recv2.at[d], to)
+        return remote(total, share.at[chip], send2, recv2, to)
 
     def gather(offset):
-        device, _, _, slot = peer(offset)
-        return remote(
-            whole, o_ref.at[own_lines, :], send3.at[slot], recv3.at[slot], device
-        )
-
-    scatters = [scatter(offset) for offset in peers]
-    exchanges = [exchange(d) for d in ring_offsets(chips)]
-    gathers = [gather(offset) for offset in peers]
-    for copy in scatters:
-        copy.start()
+        device = peer(offset)[0]
+        return remote(whole, o_ref.at[own_lines, :], send3, recv3, device)
+
+    others = 2 * n - 1
+    scattered = all_of(part.at[pl.ds(1, others)], send1, recv1)
+    exchanged = all_of(share.at[pl.ds(0, chips - 1)], send2, recv2)
+    gathered = all_of(o_ref.at[pl.ds(0, 8 * others), :], send3, recv3)
+    for offset in peers:
+        scatter(offset).start()
     part[0] = x_ref[me_p, lines(core), :]
-    for copy in scatters:
-        copy.wait_recv()
+    scattered.wait_recv()
     total[...] = jnp.sum(part[...], axis=0)
-    for copy in exchanges:
-        copy.start()
+    for d in ring_offsets(chips):
+        exchange(d).start()
     share[chip] = total[...]
-    for copy in exchanges:
-        copy.wait_recv()
+    exchanged.wait_recv()
     whole[...] = jnp.sum(share[...], axis=0)
-    for copy in gathers:
-        copy.start()
+    for offset in peers:
+        gather(offset).start()
     o_ref[own_lines, :] = whole[...]
-    for copy in gathers:
-        copy.wait_recv()
-    for copy in scatters + exchanges + gathers:
-        copy.wait_send()
+    gathered.wait_recv()
+    for stage in (scattered, exchanged, gathered):
+        stage.wait_send()
 
 
 def all_greetings():
@@ -237,9 +237,7 @@
         pltpu.VMEM(piece, jnp.float32),
         pltpu.VMEM((chips,) + piece, jnp.float32),
         pltpu.VMEM(piece, jnp.float32),
-        dma((2 * n,)), dma((2 * n,)), dma((chips,)), dma((chips,)),
-        dma((2 * n,)), dma((2 * n,)),
-    ]
+    ] + [dma] * 6
 
 
 def factor_lanes(scale, packed, tiles, state_real, state_imag):
@@ -352,11 +350,10 @@
 
     def other(offset):
         d, c = offset
-        to = lax.rem(me - core + 2 * d, n) + lax.rem(core + c, 2)
-        return to, 2 * d + c
+        return lax.rem(me - core + 2 * d, n) + lax.rem(core + c, 2)
 
     for d in ring_offsets(chips):
-        greet({"tm": other((d, 1))[0]})
+        greet({"tm": other((d, 1))})
     devices = all_greetings()
     for device in devices:
         greet(device)
@@ -370,14 +367,19 @@
 
     def travel(piece, offset):
         index, (start, width), target = piece
-        to, slot = other(offset)
+        to = other(offset)
         return remote(
             snapshots.at[:, column(to, start, width)],
             target.at[mine, :],
-            send.at[index, slot],
-            recv.at[index, slot],
+            send.at[index],
+            recv.at[index],
             {"tm": to},
         )
+
+    def arrived(piece):
+        index, _, target = piece
+        lines = target.at[pl.ds(0, SEG * (n - 1)), :]
+        return all_of(lines, send.at[index], recv.at[index])
 
     def stay(piece):
         index, (start, width), target = piece
@@ -396,8 +398,7 @@
     for piece in pieces:
         index, (start, width), target = piece
         stay(piece).wait()
-        for offset in others:
-            travel(piece, offset).wait_recv()
+        arrived(piece).wait_recv()
         panels = range(start // 128, (start + width) // 128)
         scale = jnp.sqrt(root[:, start : start + width])
 
@@ -428,8 +429,7 @@
         put_tiles(packed, group, products, False)
     sum_stages(packed, result, *sums[half:])
     for piece in pieces:
-        for offset in others:
-            travel(piece, offset).wait_send()
+        arrived(piece).wait_send()
 
 
 def first_pass(snapshots, weights, points_total):
@@ -452,8 +452,8 @@
             pltpu.VMEM(CHUNKS, jnp.float32),
             pltpu.VMEM((SEG, 6 * SEG), jnp.bfloat16),
             pltpu.VMEM((1, points), jnp.float32),
-            dma((2, n)),
-            dma((2, n)),
+            dma((2,)),
+            dma((2,)),
             dma((4,)),
             pltpu.VMEM((points // 128, TILE * LINES, 128), jnp.float32),
             pltpu.VMEM(INVERSE, jnp.float32),

time: 110 us -> 107 us (0.973)
  Pallas kernels: 109 us -> 106 us
    pallas_call x1, Pallas kernels: 100 us -> 96.9 us  [first_pass(): pl.pallas_call(lambda *refs: first_kernel(points_total, *refs), out_shape...]
where the time goes in v3:
time: 107 us
  Pallas kernels  106 us (99%)
    pallas_call x1, Pallas kernels, first_pass(): pl.pallas_call(lambda *refs: first_kernel(points_total, *refs), out_shape...  96.9 us
    pallas_call x1, Pallas kernels, finish(): pl.pallas_call(lambda *refs: finish_kernel(1.0 / points_total, *refs), ou...  8.94 us

profile of v3, /device:TPU:1, one launch (start us, length us, event | category | flops | bytes accessed | tf_op | source)
XLA Modules:
  0.0 106.6 jit_solution(5719509448151859672)
XLA Ops:
  0.6 96.9 %first_pass.1 = (f32[32,64,512]{2,1,0:T(8,128)S(1)}, f32[256,128]{1,0:T(8,128)S(1)}, f32[31,32,128]{2,1,0:T(8,128)S(1)}, f32[31,32,128]{2,1,0:T(8,128)S(1)}) custom-call(f32[64,8192]{1,0:T(8,128)} %refs_0_.1, f32[1,512]{1,0:T(1,128)} %bitcast.7, bf16[64,384]{1,0:T(8,128)(2,1)} %constant.2.clone.refs_2_), custom_call_target="tpu_custom_call" | custom-call | tf_op jit(solution)/shard_map/first_pass/pallas_call | solution.py:440
  97.5 8.9 %finish.1 = (f32[33,248,128]{2,1,0:T(8,128)}, f32[31,31,2,33]{3,2,1,0:T(2,128)}) custom-call(f32[256,128]{1,0:T(8,128)S(1)} %get-tuple-element.8.refs_0_, f32[32,64,512]{2,1,0:T(8,128)S(1)} %get-tuple-element.9.refs_1_, f32[31,32,128]{2,1,0:T(8,128)S(1)} %get-tuple-element.10.refs_2_, f32[31,32,128]{2,1,0:T(8,128)S(1)} %get-tuple-element.11.refs_3_), custom_call_target="tpu_custom_call" | custom-call | tf_op jit(solution)/shard_map/finish/pallas_call | solution.py:545

commit v4 on v3

--- a/solution.py
+++ b/solution.py
@@ -468,8 +468,7 @@
     )(*(pltpu.with_memory_space_constraint(x, pltpu.HBM) for x in inputs))
 
 
-def send_modes(ortho, inverse, modes, held, sems):
-    copies = []
+def send_modes(ortho, inverse, modes, held, sem):
     panels = ortho.shape[2] // 128
     step = 2 * panels
 
@@ -480,11 +479,7 @@
             ]
 
     def send(frequency):
-        copy = pltpu.make_async_copy(
-            held.at[frequency], modes.at[frequency], sems.at[frequency]
-        )
-        copy.start()
-        copies.append(copy)
+        pltpu.make_async_copy(held.at[frequency], modes.at[frequency], sem).start()
 
     for slot in range(SLOTS):
         value = multiply(left3(slot_matrix(inverse, slot)), right3(ortho[slot]))
@@ -498,16 +493,15 @@
             put(NF - 1, 1, nothing)
             send(NF - 1)
         send(slot)
-    return copies
 
 
 def finish_kernel(
     scale, packed, ortho, first_real, first_imag, modes, triangle,
-    held, sems, inverse, tiles, state_real, state_imag, right_real, right_imag, rows, row_sems,
+    held, sem, inverse, tiles, state_real, state_imag, right_real, right_imag, rows, row_sem,
 ):
     factor_lanes(scale, packed, tiles, state_real, state_imag)
     write_inverse(state_real, state_imag, inverse)
-    copies = send_modes(ortho, inverse, modes, held, sems)
+    send_modes(ortho, inverse, modes, held, sem)
     column = lax.broadcasted_iota(jnp.int32, (TILE, 128), 0)
     for k in range(NB):
         real = first_real[k]
@@ -532,11 +526,9 @@
             zeros = [jnp.zeros((8, 128), jnp.float32)] * (first // 8)
             line = jnp.concatenate(zeros + [total[at] for at in groups], axis=0)
             rows[i, :, part, :] = line[:NB, :NF]
-        copy = pltpu.make_async_copy(rows.at[i], triangle.at[i], row_sems.at[i])
-        copy.start()
-        copies.append(copy)
-    for copy in copies:
-        copy.wait()
+        pltpu.make_async_copy(rows.at[i], triangle.at[i], row_sem).start()
+    pltpu.make_async_copy(held, modes, sem).wait()
+    pltpu.make_async_copy(rows, triangle, row_sem).wait()
 
 
 def finish(packed, ortho, first_real, first_imag, points_total):
@@ -552,14 +544,14 @@
         out_specs=(pl.BlockSpec(memory_space=pl.ANY),) * 2,
         scratch_shapes=[
             pltpu.VMEM(shape, jnp.float32),
-            pltpu.SemaphoreType.DMA((NF,)),
+            pltpu.SemaphoreType.DMA,
             pltpu.VMEM(INVERSE, jnp.float32),
             TILES,
         ]
         + [pltpu.VMEM(STATE.shape, jnp.float32)] * 4
         + [
             pltpu.VMEM((NB, NB, 2, NF), jnp.float32),
-            pltpu.SemaphoreType.DMA((NB,)),
+            pltpu.SemaphoreType.DMA,
         ],
         compiler_params=pltpu.CompilerParams(vmem_limit_bytes=24 << 20),
         name="finish",

time: 107 us -> 106 us (level)
  no operation moved by 1% of the time
where the time goes in v4:
time: 106 us
  Pallas kernels  105 us (99%)
    pallas_call x1, Pallas kernels, first_pass(): pl.pallas_call(lambda *refs: first_kernel(points_total, *refs), out_shape...  96.9 us
    pallas_call x1, Pallas kernels, finish(): pl.pallas_call(lambda *refs: finish_kernel(1.0 / points_total, *refs), ou...  8.33 us

profile of v4, /device:TPU:1, one launch (start us, length us, event | category | flops | bytes accessed | tf_op | source)
XLA Modules:
  0.0 106.0 jit_solution(16010834476409396129)
XLA Ops:
  0.6 96.9 %first_pass.1 = (f32[32,64,512]{2,1,0:T(8,128)S(1)}, f32[256,128]{1,0:T(8,128)S(1)}, f32[31,32,128]{2,1,0:T(8,128)S(1)}, f32[31,32,128]{2,1,0:T(8,128)S(1)}) custom-call(f32[64,8192]{1,0:T(8,128)} %refs_0_.1, f32[1,512]{1,0:T(1,128)} %bitcast.7, bf16[64,384]{1,0:T(8,128)(2,1)} %constant.2.clone.refs_2_), custom_call_target="tpu_custom_call" | custom-call | tf_op jit(solution)/shard_map/first_pass/pallas_call | solution.py:440
  97.5 8.3 %finish.1 = (f32[33,248,128]{2,1,0:T(8,128)}, f32[31,31,2,33]{3,2,1,0:T(2,128)}) custom-call(f32[256,128]{1,0:T(8,128)S(1)} %get-tuple-element.8.refs_0_, f32[32,64,512]{2,1,0:T(8,128)S(1)} %get-tuple-element.9.refs_1_, f32[31,32,128]{2,1,0:T(8,128)S(1)} %get-tuple-element.10.refs_2_, f32[31,32,128]{2,1,0:T(8,128)S(1)} %get-tuple-element.11.refs_3_), custom_call_target="tpu_custom_call" | custom-call | tf_op jit(solution)/shard_map/finish/pallas_call | solution.py:537
